TPU v7x, 128 devices: a whole 4x4x4 slice. The times are simulated.
128 devices in a mesh: row: 8 (over x, core), col: 16 (over y, z).
Axes of the slice: x: 4, y: 4, z: 4, core: 2. Of those that a mesh axis runs over, the one named last changes fastest.
Arguments:
- factor: float32 [4, 8, 1024, 2048], P(None, 'row', None, 'col'), as said below
- cross_cov: float32 [4, 8, 1024, 1024], P(None, 'row', 'col'), may hold values from -6 to 6
Outputs:
- overwritten: float32 [4, 8, 1024, 1024], P(None, 'row', 'col')
Inputs may be any that keep to these rules, and one draw needn't show every extreme that they name: The diagonal entries of the factor lie between 1 and 3.
All inputs are finite; a program needn't handle non-finite values.
Results may differ from a plain program's by a relative error of at most 0.00014.
Values sent between devices are 32-bit elements; how exact they have to be, the bound alone decides.
No kernel may reach another device: no remote copies, remote signals or barrier semaphores. Data moves between devices by JAX's collectives and lax.ppermute only.
A program may use at most 128 MiB of HBM per device.

v0:
```python
import jax
import jax.numpy as jnp
from jax import lax
from jax.sharding import PartitionSpec as P


def broadcast(x, axis, root):
    mine = lax.axis_index(axis) == root
    return lax.psum(jnp.where(mine, x, jnp.zeros_like(x)), axis)


def spread(block, root):
    return broadcast(block, "row", root)


def reduce_turn(partial_value):
    return lax.psum_scatter(partial_value, "col", scatter_dimension=0, tiled=True)


def shards(factor, cross_cov):
    col_id = lax.axis_index("col")
    row_id = lax.axis_index("row")
    lead_rows = factor[0, 0]
    own_rhs = cross_cov[0, 0]
    block_row, block_rhs = (
        lax.all_gather(lead_rows, "col", axis=1, tiled=True),
        lax.all_gather(own_rhs, "col", axis=0, tiled=True),
    )
    block_size = block_row.shape[0]
    first_block = lax.linalg.triangular_solve(
        block_row[:, :block_size], block_rhs, left_side=True, lower=True
    )
    first_block = spread(first_block, 0)
    second_rhs = block_rhs - jnp.dot(
        block_row[:, :block_size], first_block, precision=lax.Precision.HIGHEST
    )
    second_block = lax.linalg.triangular_solve(
        block_row[:, block_size:], second_rhs, left_side=True, lower=True
    )
    second_block = spread(second_block, 1)
    solved = jnp.concatenate([first_block, second_block], 0)
    local_factor = factor[:, 0]
    col_width = local_factor.shape[2]
    my_rows = lax.dynamic_slice_in_dim(solved, col_id * col_width, col_width, 0)
    pieces = []
    for turn_id in range(local_factor.shape[0]):
        partial_value = jnp.dot(local_factor[turn_id], my_rows, precision=lax.Precision.HIGHEST)
        pieces.append(reduce_turn(partial_value))
    reduced = jnp.stack(pieces, 0)
    updated = cross_cov[:, 0] - reduced
    slice_rows = own_rhs.shape[0]
    first_piece = lax.dynamic_slice_in_dim(first_block, col_id * slice_rows, slice_rows, 0)
    second_piece = lax.dynamic_slice_in_dim(second_block, col_id * slice_rows, slice_rows, 0)
    head_rows = jnp.where(
        row_id == 0, first_piece, jnp.where(row_id == 1, second_piece, updated[0])
    )
    result = jnp.concatenate([head_rows[None], updated[1:]], 0)
    return result[:, None]


def solution(mesh):
    placed = (P(None, "row", None, "col"), P(None, "row", "col", None))
    return jax.shard_map(
        shards, mesh=mesh, in_specs=placed, out_specs=P(None, "row", "col", None), check_vma=False
    )
```

profile of v0, /device:TPU:0, one launch (start us, length us, event | category | flops | bytes accessed | tf_op | source)
XLA Modules:
  0.0 875.4 jit_solution(348379081481082438)
XLA Ops:
  10.5 53.1 %all-gather.7.cloned.1.call-done = f32[1,1,1024,1024]{3,1,0,2:T(1,128)} async-done(((f32[1,1,64,1024]{3,1,0,2:T(1,128)}), f32[1,1,1024,1024]{3,1,0,2:T(1,128)}) %all-gather.7.cloned.1.call-update) | async-done | bytes 4194320 | tf_op jit(solution)/shard_map/all_gather | solution.py:27
  63.7 11.0 %copy.10 = f32[1,1,1024,1024]{2,3,1,0:T(8,128)} copy(f32[1,1,1024,1024]{3,1,0,2:T(1,128)} %all-gather.7.cloned.1.call-done) | data formatting | bytes 8388608 | tf_op jit(solution)/shard_map/all_gather | solution.py:27
  74.7 69.2 %all-gather.5.cloned.1.call-done = f32[1,1,1024,2048]{3,2,1,0:T(8,128)} async-done(((f32[1,1,1024,128]{3,2,1,0:T(8,128)}), f32[1,1,1024,2048]{3,2,1,0:T(8,128)}) %all-gather.5.cloned.1.call-update) | async-done | bytes 8388624 | tf_op jit(solution)/shard_map/all_gather | solution.py:26
  143.9 8.0 slice_select_fusion
  151.9 22.5 %while.4 = (s32[]{:T(128)}, f32[1024,1024]{1,0:T(8,128)}, s32[8,2]{0,1:T(2,128)S(1)}, f32[8,128,128]{2,1,0:T(8,128)S(1)}, s32[]{:T(128)}) while((s32[]{:T(128)}, f32[1024,1024]{1,0:T(8,128)}, s32[8,2]{0,1:T(2,128)S(1)}, f32[8,128,128]{2,1,0:T(8,128)S(1)}, s32[]{:T(128)}) %tuple.80), condition=%wide.while_cond, body=%wide.while_body.sunk | while | flops 2 | bytes 131181 | solution.py:30
  152.5 2.2 bitcast_dynamic-update-slice_fusion.4
  155.3 2.2 bitcast_dynamic-update-slice_fusion.4
  158.2 2.2 bitcast_dynamic-update-slice_fusion.4
  161.0 2.2 bitcast_dynamic-update-slice_fusion.4
  163.8 2.2 bitcast_dynamic-update-slice_fusion.4
  166.6 2.2 bitcast_dynamic-update-slice_fusion.4
  169.4 2.2 bitcast_dynamic-update-slice_fusion.4
  172.3 2.1 bitcast_dynamic-update-slice_fusion.4
  174.4 78.8 %custom-call.4 = f32[8,128,128]{1,2,0:T(8,128)S(1)} custom-call(f32[8,128,128]{2,1,0:T(8,128)S(1)} %get-tuple-element.20), custom_call_target="InvertDiagBlocksLowerTriangular" | custom-call | tf_op jit(solution)/shard_map/triangular_solve/custom-call.1 | solution.py:30
  258.0 2.7 convolution_subtract_fusion.1
  261.5 3.7 fusion.36
  266.0 4.4 fusion.42
  271.3 5.4 convolution_subtract_fusion.5
  277.4 6.0 convolution_subtract_fusion.3
  284.1 7.5 convolution_subtract_fusion.8
  292.3 2.5 broadcast_select_fusion.1
  294.8 22.5 %while.5 = (s32[]{:T(128)}, f32[1024,1024]{1,0:T(8,128)}, s32[8,2]{0,1:T(2,128)S(1)}, f32[8,128,128]{2,1,0:T(8,128)S(1)}, s32[]{:T(128)}) while((s32[]{:T(128)}, f32[1024,1024]{1,0:T(8,128)}, s32[8,2]{0,1:T(2,128)S(1)}, f32[8,128,128]{2,1,0:T(8,128)S(1)}, s32[]{:T(128)}) %tuple.102), condition=%wide.while_cond.clone, body=%wide.while_body.clone.sunk | while | flops 2 | bytes 131181 | solution.py:37
  295.4 2.2 bitcast_dynamic-update-slice_fusion.5
  298.3 2.2 bitcast_dynamic-update-slice_fusion.5
  301.1 2.2 bitcast_dynamic-update-slice_fusion.5
  303.9 2.2 bitcast_dynamic-update-slice_fusion.5
  306.7 2.2 bitcast_dynamic-update-slice_fusion.5
  309.5 2.2 bitcast_dynamic-update-slice_fusion.5
  312.3 2.2 bitcast_dynamic-update-slice_fusion.5
  315.2 2.1 bitcast_dynamic-update-slice_fusion.5
  317.3 78.6 %custom-call.5 = f32[8,128,128]{1,2,0:T(8,128)S(1)} custom-call(f32[8,128,128]{2,1,0:T(8,128)S(1)} %get-tuple-element.21), custom_call_target="InvertDiagBlocksLowerTriangular" | custom-call | tf_op jit(solution)/shard_map/triangular_solve/custom-call.1 | solution.py:37
  395.9 30.9 %bitcast_subtract_fusion = f32[1024,1024]{0,1:T(8,128)S(1)} fusion(f32[1024,1024]{1,0:T(8,128)} %all-reduce.3.cloned.1.call-done, f32[1024,2048]{1,0:T(8,128)} %bitcast.173, f32[1,1,1024,1024]{2,3,1,0:T(8,128)} %copy.10), kind=kOutput, calls=%fused_computation.7 | convolution fusion | flops 12885950464 | bytes 16777216 | tf_op jit(solution)/shard_map/dot_general | solution.py:34
  430.2 2.8 convolution_subtract_fusion
  433.7 3.7 fusion.33
  438.1 4.4 fusion.39
  443.5 5.4 convolution_subtract_fusion.4
  449.5 6.2 convolution_subtract_fusion.2
  456.3 7.3 convolution_subtract_fusion.6
  464.4 2.5 broadcast_select_fusion
  466.9 71.9 %all-reduce.5.cloned.1.call-done = f32[1024,1024]{1,0:T(8,128)} async-done(((f32[1024,1024]{1,0:T(8,128)}), f32[1024,1024]{1,0:T(8,128)}) %all-reduce.5.cloned.1.call-update) | async-done | bytes 4194320 | tf_op jit(solution)/shard_map/psum | solution.py:9
  538.8 6.2 convolution_bitcast_fusion.3
  545.1 6.1 convolution_bitcast_fusion.2
  551.3 6.1 convolution_bitcast_fusion.1
  557.5 6.2 convolution_bitcast_fusion
  563.7 59.3 %reduce-scatter.5.cloned.1.call-done = f32[64,1024]{1,0:T(8,128)} async-done(((f32[1024,1024]{1,0:T(8,128)}), f32[64,1024]{1,0:T(8,128)}) %reduce-scatter.5.cloned.1.call-update) | async-done | bytes 262160 | tf_op jit(solution)/shard_map/reduce_scatter | solution.py:17
  623.1 80.6 %reduce-scatter.7.cloned.1.call-done = f32[64,1024]{1,0:T(8,128)} async-done(((f32[1024,1024]{1,0:T(8,128)}), f32[64,1024]{1,0:T(8,128)}) %reduce-scatter.7.cloned.1.call-update) | async-done | bytes 262160 | tf_op jit(solution)/shard_map/reduce_scatter | solution.py:17
  703.7 80.4 %reduce-scatter.9.cloned.1.call-done = f32[64,1024]{1,0:T(8,128)} async-done(((f32[1024,1024]{1,0:T(8,128)}), f32[64,1024]{1,0:T(8,128)}) %reduce-scatter.9.cloned.1.call-update) | async-done | bytes 262160 | tf_op jit(solution)/shard_map/reduce_scatter | solution.py:17
  784.0 80.7 %reduce-scatter.11.cloned.1.call-done = f32[64,1024]{1,0:T(8,128)} async-done(((f32[1024,1024]{1,0:T(8,128)}), f32[64,1024]{1,0:T(8,128)}) %reduce-scatter.11.cloned.1.call-update) | async-done | bytes 262160 | tf_op jit(solution)/shard_map/reduce_scatter | solution.py:17
  (84 shorter events, 34.4 us)
Async XLA Ops:
  6.5 57.1 %all-gather.7.cloned.1.call-start = ((), (), s32[]{:S(2)}) async-start(), calls=%async_computation.11 | async-start | bytes 4456448 | tf_op jit(solution)/shard_map/all_gather | solution.py:27
  8.5 135.4 %all-gather.5.cloned.1.call-start = ((), (), s32[]{:S(2)}) async-start(), calls=%async_computation.10 | async-start | bytes 8912896 | tf_op jit(solution)/shard_map/all_gather | solution.py:26
  10.5 385.5 %all-reduce.3.cloned.1.call-start = ((), (), s32[]{:S(2)}) async-start(), calls=%async_computation.4 | async-start | bytes 8388608 | tf_op jit(solution)/shard_map/psum | solution.py:9
  253.2 4.8 copy-start
  294.7 244.1 %all-reduce.5.cloned.1.call-start = ((), (), s32[]{:S(2)}) async-start(), calls=%async_computation.5 | async-start | bytes 8388608 | tf_op jit(solution)/shard_map/psum | solution.py:9
  466.8 72.0 %copy-start.1 = (f32[4,1,1024,128]{3,2,1,0:T(8,128)S(1)}, f32[4,1,1024,128]{3,2,1,0:T(8,128)}, u32[]{:S(2)}) copy-start(f32[4,1,1024,128]{3,2,1,0:T(8,128)} %param.4) | copy-start | bytes 6291460
  466.8 156.2 %reduce-scatter.5.cloned.1.call-start = ((), (), s32[]{:S(2)}) async-start(), calls=%async_computation.6 | async-start | bytes 4456448 | tf_op jit(solution)/shard_map/reduce_scatter | solution.py:17
  545.0 158.6 %reduce-scatter.7.cloned.1.call-start = ((), (), s32[]{:S(2)}) async-start(), calls=%async_computation.7 | async-start | bytes 4456448 | tf_op jit(solution)/shard_map/reduce_scatter | solution.py:17
  551.2 232.8 %reduce-scatter.9.cloned.1.call-start = ((), (), s32[]{:S(2)}) async-start(), calls=%async_computation.8 | async-start | bytes 4456448 | tf_op jit(solution)/shard_map/reduce_scatter | solution.py:17
  557.4 307.3 %reduce-scatter.11.cloned.1.call-start = ((), (), s32[]{:S(2)}) async-start(), calls=%async_computation.9 | async-start | bytes 4456448 | tf_op jit(solution)/shard_map/reduce_scatter | solution.py:17
  563.7 301.1 %copy-start.2 = (f32[4,1,64,1024]{3,2,1,0:T(8,128)S(1)}, f32[4,1,64,1024]{3,2,1,0:T(8,128)}, u32[]{:S(2)}) copy-start(f32[4,1,64,1024]{3,2,1,0:T(8,128)} %param.5) | copy-start | bytes 3145732
Sparse Core Ops, SparseCore 0:
  9.5 54.1 all-gather.6
  65.8 78.0 all-gather.4
  294.9 73.0 all-reduce.2
  467.0 71.7 all-reduce.4
  545.1 77.8 reduce-scatter.4
  626.6 77.0 reduce-scatter.6
  707.0 76.9 reduce-scatter.8
  787.7 77.0 reduce-scatter.10
where the time goes:
time: 880 us; the launch traced here: 875 us
  waiting for transfers between devices  495 us (56%)
  other arithmetic  174 us (20%)
  matrix products  132 us (15%)
  local copies, waits for them, and re-layouts  59.6 us (7%)
  between operations  14.1 us (2%)
    reduce_scatter x4, waiting for transfers between devices, reduce_turn(): lax.psum_scatter(partial_value, 'col', scatter_dimension=0, tiled=True)  301 us
    another operation x2, other arithmetic, shards(): lax.linalg.triangular_solve(block_row[:, block_size:], second_rhs, left_s...  86.6 us
    another operation x2, other arithmetic, shards(): lax.linalg.triangular_solve(block_row[:, :block_size], block_rhs, left_si...  78.8 us
    psum x2, waiting for transfers between devices, broadcast(): return lax.psum(jnp.where(mine, x, jnp.zeros_like(x)), axis)  71.9 us
    all_gather x1, waiting for transfers between devices, shards(): lax.all_gather(lead_rows, 'col', axis=1, tiled=True)  69.2 us
    all_gather x1, waiting for transfers between devices, shards(): lax.all_gather(own_rhs, 'col', axis=0, tiled=True)  53.1 us
    another operation x15, matrix products, shards(): lax.linalg.triangular_solve(block_row[:, :block_size], block_rhs, left_si...  38.9 us
    another operation x15, matrix products, shards(): lax.linalg.triangular_solve(block_row[:, block_size:], second_rhs, left_s...  37.4 us
  transfers between devices with their start and end apart: 8, of which 7 were waited for; matrix products, arithmetic and copies ran while one was open for 15% of the time, Pallas kernels for 0%

commit v1 on v0

--- a/solution.py
+++ b/solution.py
@@ -2,6 +2,27 @@
 import jax.numpy as jnp
 from jax import lax
 from jax.sharding import PartitionSpec as P
+
+
+def ring_gather(x, axis, dim):
+    devices, index, rows = (lax.axis_size(axis), lax.axis_index(axis), x.shape[dim])
+    forward = [(i, (i + 1) % devices) for i in range(devices)]
+    downward = [(i, (i - 1) % devices) for i in range(devices)]
+    whole = jnp.zeros((*x.shape[:dim], devices * rows, *x.shape[dim + 1 :]), x.dtype)
+    whole = lax.dynamic_update_slice_in_dim(whole, x, index * rows, axis=dim)
+    from_left = from_right = x
+    halfway = devices // 2
+    for hop in range(1, halfway + 1):
+        from_left = lax.ppermute(from_left, axis, forward)
+        whole = lax.dynamic_update_slice_in_dim(
+            whole, from_left, (index - hop) % devices * rows, axis=dim
+        )
+        if hop < devices - halfway:
+            from_right = lax.ppermute(from_right, axis, downward)
+            whole = lax.dynamic_update_slice_in_dim(
+                whole, from_right, (index + hop) % devices * rows, axis=dim
+            )
+    return whole
 
 
 def broadcast(x, axis, root):
@@ -23,7 +44,7 @@
     lead_rows = factor[0, 0]
     own_rhs = cross_cov[0, 0]
     block_row, block_rhs = (
-        lax.all_gather(lead_rows, "col", axis=1, tiled=True),
+        ring_gather(lead_rows, "col", 1),
         lax.all_gather(own_rhs, "col", axis=0, tiled=True),
     )
     block_size = block_row.shape[0]

time: 880 us -> 839 us (0.953)
  waiting for transfers between devices: 495 us -> 435 us
  matrix products: 132 us -> 88.3 us
  starting transfers between devices: 0.29 us -> 41.1 us
  local copies, waits for them, and re-layouts: 59.6 us -> 77.9 us
    all_gather x1 -> x0, waiting for transfers between devices: 69.2 us -> none  [shards(): lax.all_gather(lead_rows, 'col', axis=1, tiled=True)]
    ppermute x0 -> x15, waiting for transfers between devices: none -> 64.8 us  [the longest x8 54.8 us: ring_gather(): from_left = lax.ppermute(from_left, axis, forward)]
    all_gather x1, waiting for transfers between devices: 53.1 us -> 0.02 us  [shards(): lax.all_gather(own_rhs, 'col', axis=0, tiled=True)]
    ppermute x0 -> x15, starting transfers between devices: none -> 40.8 us  [the longest x7 38.7 us: ring_gather(): from_right = lax.ppermute(from_right, axis, downward)]
    dynamic_update_slice x0 -> x16, local copies, waits for them, and re-layouts: none -> 23.6 us  [the longest x7 11.4 us: ring_gather(): lax.dynamic_update_slice_in_dim(whole, from_right, (index + hop) % device...]
    another operation x15, matrix products: 38.9 us -> 23.3 us  [shards(): lax.linalg.triangular_solve(block_row[:, :block_size], block_rhs, left_si...]
    another operation x15, matrix products: 37.4 us -> 22 us  [shards(): lax.linalg.triangular_solve(block_row[:, block_size:], second_rhs, left_s...]
    dot_general x1, matrix products: 30.9 us -> 18.3 us  [shards(): jnp.dot(block_row[:, :block_size], first_block, precision=lax.Precision.H...]
  transfers between devices with their start and end apart: 8 -> 22, of which waited for: 7 -> 15; matrix products, arithmetic and copies ran while one was open for 15% -> 31% of each run, Pallas kernels for 0% -> 0%
where the time goes in v1:
time: 839 us; the launch traced here: 830 us
  waiting for transfers between devices  435 us (52%)
  other arithmetic  174 us (21%)
  matrix products  88.3 us (11%)
  local copies, waits for them, and re-layouts  77.9 us (9%)
  starting transfers between devices  41.1 us (5%)
  between operations  14 us (2%)
    reduce_scatter x4, waiting for transfers between devices, reduce_turn(): lax.psum_scatter(partial_value, 'col', scatter_dimension=0, tiled=True)  301 us
    another operation x2, other arithmetic, shards(): lax.linalg.triangular_solve(block_row[:, block_size:], second_rhs, left_s...  86.5 us
    another operation x2, other arithmetic, shards(): lax.linalg.triangular_solve(block_row[:, :block_size], block_rhs, left_si...  78.8 us
    psum x2, waiting for transfers between devices, broadcast(): return lax.psum(jnp.where(mine, x, jnp.zeros_like(x)), axis)  69 us
    ppermute x8, waiting for transfers between devices, ring_gather(): from_left = lax.ppermute(from_left, axis, forward)  54.8 us
    ppermute x7, starting transfers between devices, ring_gather(): from_right = lax.ppermute(from_right, axis, downward)  38.7 us
    dot_general x4, matrix products, shards(): jnp.dot(local_factor[turn_id], my_rows, precision=lax.Precision.HIGHEST)  24.8 us
    another operation x24, local copies, waits for them, and re-layouts, shards(): lax.linalg.triangular_solve(block_row[:, block_size:], second_rhs, left_s...  24 us
  transfers between devices with their start and end apart: 22, of which 15 were waited for; matrix products, arithmetic and copies ran while one was open for 31% of the time, Pallas kernels for 0%

profile of v1, /device:TPU:0, one launch (start us, length us, event | category | flops | bytes accessed | tf_op | source)
XLA Modules:
  0.0 830.0 jit_solution(14582387666143403638)
XLA Ops:
  11.4 4.7 collective-permute-start.1
  16.1 10.1 %collective-permute-done = f32[1024,128]{1,0:T(8,128)S(1)} collective-permute-done((f32[1024,128]{1,0:T(8,128)S(1)}, f32[1024,128]{1,0:T(8,128)S(1)}, u32[]{:S(2)}, u32[]{:S(2)}) %collective-permute-start) | collective-permute-done | bytes 524320 | tf_op jit(solution)/shard_map/ppermute | solution.py:16
  26.2 2.7 collective-permute-done.1
  28.9 5.8 collective-permute-start.3
  34.7 10.7 %collective-permute-done.2 = f32[1024,128]{1,0:T(8,128)S(1)} collective-permute-done((f32[1024,128]{1,0:T(8,128)S(1)}, f32[1024,128]{1,0:T(8,128)S(1)}, u32[]{:S(2)}, u32[]{:S(2)}) %collective-permute-start.2) | collective-permute-done | bytes 524320 | tf_op jit(solution)/shard_map/ppermute | solution.py:16
  45.7 5.8 collective-permute-start.5
  51.5 13.5 %collective-permute-done.4 = f32[1024,128]{1,0:T(8,128)S(1)} collective-permute-done((f32[1024,128]{1,0:T(8,128)S(1)}, f32[1024,128]{1,0:T(8,128)S(1)}, u32[]{:S(2)}, u32[]{:S(2)}) %collective-permute-start.4) | collective-permute-done | bytes 524320 | tf_op jit(solution)/shard_map/ppermute | solution.py:16
  65.0 7.0 collective-permute-done.5
  72.1 5.9 collective-permute-start.7
  78.0 11.5 %collective-permute-done.6 = f32[1024,128]{1,0:T(8,128)} collective-permute-done((f32[1024,128]{1,0:T(8,128)S(1)}, f32[1024,128]{1,0:T(8,128)}, u32[]{:S(2)}, u32[]{:S(2)}) %collective-permute-start.6) | collective-permute-done | bytes 524320 | tf_op jit(solution)/shard_map/ppermute | solution.py:16
  89.6 5.9 collective-permute-start.9
  95.4 4.3 broadcast_in_dim.9
  107.6 5.4 collective-permute-start.11
  122.3 5.3 collective-permute-start.13
  136.0 6.0 collective-permute-done.14
  143.0 7.9 slice_select_fusion
  150.9 23.2 %while.4 = (s32[]{:T(128)}, f32[1024,1024]{1,0:T(8,128)}, s32[8,2]{0,1:T(2,128)S(1)}, f32[8,128,128]{2,1,0:T(8,128)S(1)}, s32[]{:T(128)}) while((s32[]{:T(128)}, f32[1024,1024]{1,0:T(8,128)}, s32[8,2]{0,1:T(2,128)S(1)}, f32[8,128,128]{2,1,0:T(8,128)S(1)}, s32[]{:T(128)}) %tuple.80), condition=%wide.while_cond, body=%wide.while_body.sunk | while | flops 2 | bytes 131181 | solution.py:51
  154.4 2.3 bitcast_dynamic-update-slice_fusion.4
  160.3 2.3 bitcast_dynamic-update-slice_fusion.4
  166.1 2.3 bitcast_dynamic-update-slice_fusion.4
  174.1 78.8 %custom-call.4 = f32[8,128,128]{1,2,0:T(8,128)S(1)} custom-call(f32[8,128,128]{2,1,0:T(8,128)S(1)} %get-tuple-element.20), custom_call_target="InvertDiagBlocksLowerTriangular" | custom-call | tf_op jit(solution)/shard_map/triangular_solve/custom-call.1 | solution.py:51
  265.4 2.6 convolution_subtract_fusion.2
  268.7 2.8 convolution_subtract_fusion.1
  272.2 3.5 convolution_subtract_fusion.3
  276.3 2.5 broadcast_select_fusion.1
  278.9 24.2 %while.5 = (s32[]{:T(128)}, f32[1024,1024]{1,0:T(8,128)}, s32[8,2]{0,1:T(2,128)S(1)}, f32[8,128,128]{2,1,0:T(8,128)S(1)}, s32[]{:T(128)}) while((s32[]{:T(128)}, f32[1024,1024]{1,0:T(8,128)}, s32[8,2]{0,1:T(2,128)S(1)}, f32[8,128,128]{2,1,0:T(8,128)S(1)}, s32[]{:T(128)}) %tuple.100), condition=%wide.while_cond.clone, body=%wide.while_body.clone.sunk | while | flops 2 | bytes 131181 | solution.py:58
  279.6 2.3 bitcast_dynamic-update-slice_fusion.5
  282.6 2.3 bitcast_dynamic-update-slice_fusion.5
  285.7 2.3 bitcast_dynamic-update-slice_fusion.5
  288.7 2.3 bitcast_dynamic-update-slice_fusion.5
  291.7 2.3 bitcast_dynamic-update-slice_fusion.5
  294.7 2.3 bitcast_dynamic-update-slice_fusion.5
  297.8 2.3 bitcast_dynamic-update-slice_fusion.5
  303.1 78.6 %custom-call.5 = f32[8,128,128]{1,2,0:T(8,128)S(1)} custom-call(f32[8,128,128]{2,1,0:T(8,128)S(1)} %get-tuple-element.21), custom_call_target="InvertDiagBlocksLowerTriangular" | custom-call | tf_op jit(solution)/shard_map/triangular_solve/custom-call.1 | solution.py:58
  381.7 18.3 %fusion.19 = f32[1024,1024]{1,0:T(8,128)S(1)} fusion(f32[1024,1024]{1,0:T(8,128)} %all-reduce.3.cloned.1.call-done, f32[1024,2048]{1,0:T(8,128)} %constant_dynamic-update-slice_fusion.50, f32[1,1,1024,1024]{3,2,1,0:T(8,128)} %all-gather.3.cloned.1.call-done), kind=kOutput, calls=%fused_computation.33 | convolution fusion | flops 12885950464 | bytes 16777216 | tf_op jit(solution)/shard_map/dot_general | solution.py:55
  411.1 2.6 fusion.70
  414.5 2.8 fusion.67
  418.0 3.4 fusion.64
  422.1 2.5 broadcast_select_fusion
  424.6 69.0 %all-reduce.5.cloned.1.call-done = f32[1024,1024]{1,0:T(8,128)} async-done(((f32[1024,1024]{1,0:T(8,128)}), f32[1024,1024]{1,0:T(8,128)}) %all-reduce.5.cloned.1.call-update) | async-done | bytes 4194320 | tf_op jit(solution)/shard_map/psum | solution.py:30
  493.6 6.2 convolution_bitcast_fusion.3
  499.9 6.2 convolution_bitcast_fusion.2
  506.1 6.1 convolution_bitcast_fusion.1
  512.4 6.2 convolution_bitcast_fusion
  518.6 59.2 %reduce-scatter.5.cloned.1.call-done = f32[64,1024]{1,0:T(8,128)} async-done(((f32[1024,1024]{1,0:T(8,128)}), f32[64,1024]{1,0:T(8,128)}) %reduce-scatter.5.cloned.1.call-update) | async-done | bytes 262160 | tf_op jit(solution)/shard_map/reduce_scatter | solution.py:38
  577.8 80.6 %reduce-scatter.7.cloned.1.call-done = f32[64,1024]{1,0:T(8,128)} async-done(((f32[1024,1024]{1,0:T(8,128)}), f32[64,1024]{1,0:T(8,128)}) %reduce-scatter.7.cloned.1.call-update) | async-done | bytes 262160 | tf_op jit(solution)/shard_map/reduce_scatter | solution.py:38
  658.4 80.3 %reduce-scatter.9.cloned.1.call-done = f32[64,1024]{1,0:T(8,128)} async-done(((f32[1024,1024]{1,0:T(8,128)}), f32[64,1024]{1,0:T(8,128)}) %reduce-scatter.9.cloned.1.call-update) | async-done | bytes 262160 | tf_op jit(solution)/shard_map/reduce_scatter | solution.py:38
  738.6 80.8 %reduce-scatter.11.cloned.1.call-done = f32[64,1024]{1,0:T(8,128)} async-done(((f32[1024,1024]{1,0:T(8,128)}), f32[64,1024]{1,0:T(8,128)}) %reduce-scatter.11.cloned.1.call-update) | async-done | bytes 262160 | tf_op jit(solution)/shard_map/reduce_scatter | solution.py:38
  (132 shorter events, 86.9 us)
Async XLA Ops:
  6.5 246.4 %all-gather.3.cloned.1.call-start = ((), (), s32[]{:S(2)}) async-start(), calls=%async_computation.10 | async-start | bytes 4456448 | tf_op jit(solution)/shard_map/all_gather | solution.py:48
  7.6 18.6 %collective-permute-start = (f32[1024,128]{1,0:T(8,128)S(1)}, f32[1024,128]{1,0:T(8,128)S(1)}, u32[]{:S(2)}, u32[]{:S(2)}) collective-permute-start(f32[1024,128]{1,0:T(8,128)S(1)} %slice_bitcast_fusion), channel_id=1, source_target_pairs={{0,1},{1,2},{2,3},{3,4},{4,5},{5,6},{6,7},{7,8},{8,9},{9,10},{10,1... | collective-permute-start | bytes 1572872 | tf_op jit(solution)/shard_map/ppermute | solution.py:16
  11.4 370.3 %all-reduce.3.cloned.1.call-start = ((), (), s32[]{:S(2)}) async-start(), calls=%async_computation.4 | async-start | bytes 8388608 | tf_op jit(solution)/shard_map/psum | solution.py:30
  11.4 17.4 %collective-permute-start.1 = (f32[1024,128]{1,0:T(8,128)S(1)}, f32[1024,128]{1,0:T(8,128)S(1)}, u32[]{:S(2)}, u32[]{:S(2)}) collective-permute-start(f32[1024,128]{1,0:T(8,128)S(1)} %slice_bitcast_fusion), channel_id=1, source_target_pairs={{0,15},{1,0},{2,1},{3,2},{4,3},{5,4},{6,5},{7,6},{8,7},{9,8},{10,9... | collective-permute-start | bytes 1572872 | tf_op jit(solution)/shard_map/ppermute | solution.py:21
  26.2 19.2 %collective-permute-start.2 = (f32[1024,128]{1,0:T(8,128)S(1)}, f32[1024,128]{1,0:T(8,128)S(1)}, u32[]{:S(2)}, u32[]{:S(2)}) collective-permute-start(f32[1024,128]{1,0:T(8,128)S(1)} %collective-permute-done), channel_id=1, source_target_pairs={{0,1},{1,2},{2,3},{3,4},{4,5},{5,6},{6,7},{7,8},{8,9},{9,10},{10,1... | collective-permute-start | bytes 1572872 | tf_op jit(solution)/shard_map/ppermute | solution.py:16
  28.9 60.6 %copy-start.3 = (f32[1024,128]{1,0:T(8,128)}, f32[1024,128]{1,0:T(8,128)S(1)}, u32[]{:S(2)}) copy-start(f32[1024,128]{1,0:T(8,128)S(1)} %collective-permute-done.1) | copy-start | bytes 1572868
  28.9 16.8 %collective-permute-start.3 = (f32[1024,128]{1,0:T(8,128)S(1)}, f32[1024,128]{1,0:T(8,128)S(1)}, u32[]{:S(2)}, u32[]{:S(2)}) collective-permute-start(f32[1024,128]{1,0:T(8,128)S(1)} %collective-permute-done.1), channel_id=1, source_target_pairs={{0,15},{1,0},{2,1},{3,2},{4,3},{5,4},{6,5},{7,6},{8,7},{9,8},{10,9... | collective-permute-start | bytes 1572872 | tf_op jit(solution)/shard_map/ppermute | solution.py:21
  45.4 44.1 %copy-start.5 = (f32[1024,128]{1,0:T(8,128)}, f32[1024,128]{1,0:T(8,128)S(1)}, u32[]{:S(2)}) copy-start(f32[1024,128]{1,0:T(8,128)S(1)} %collective-permute-done.2) | copy-start | bytes 1572868
  45.4 19.6 %collective-permute-start.4 = (f32[1024,128]{1,0:T(8,128)S(1)}, f32[1024,128]{1,0:T(8,128)S(1)}, u32[]{:S(2)}, u32[]{:S(2)}) collective-permute-start(f32[1024,128]{1,0:T(8,128)S(1)} %collective-permute-done.2), channel_id=1, source_target_pairs={{0,1},{1,2},{2,3},{3,4},{4,5},{5,6},{6,7},{7,8},{8,9},{9,10},{10,1... | collective-permute-start | bytes 1572872 | tf_op jit(solution)/shard_map/ppermute | solution.py:16
  45.7 43.8 %copy-start.4 = (f32[1024,128]{1,0:T(8,128)}, f32[1024,128]{1,0:T(8,128)S(1)}, u32[]{:S(2)}) copy-start(f32[1024,128]{1,0:T(8,128)S(1)} %collective-permute-done.3) | copy-start | bytes 1572868
  45.7 26.4 %collective-permute-start.5 = (f32[1024,128]{1,0:T(8,128)S(1)}, f32[1024,128]{1,0:T(8,128)}, u32[]{:S(2)}, u32[]{:S(2)}) collective-permute-start(f32[1024,128]{1,0:T(8,128)S(1)} %collective-permute-done.3), channel_id=1, source_target_pairs={{0,15},{1,0},{2,1},{3,2},{4,3},{5,4},{6,5},{7,6},{8,7},{9,8},{10,9... | collective-permute-start | bytes 1572872 | tf_op jit(solution)/shard_map/ppermute | solution.py:21
  65.0 24.5 %collective-permute-start.6 = (f32[1024,128]{1,0:T(8,128)S(1)}, f32[1024,128]{1,0:T(8,128)}, u32[]{:S(2)}, u32[]{:S(2)}) collective-permute-start(f32[1024,128]{1,0:T(8,128)S(1)} %collective-permute-done.4), channel_id=1, source_target_pairs={{0,1},{1,2},{2,3},{3,4},{4,5},{5,6},{6,7},{7,8},{8,9},{9,10},{10,1... | collective-permute-start | bytes 1572872 | tf_op jit(solution)/shard_map/ppermute | solution.py:16
  72.1 17.5 %collective-permute-start.7 = (f32[1024,128]{1,0:T(8,128)}, f32[1024,128]{1,0:T(8,128)}, u32[]{:S(2)}, u32[]{:S(2)}) collective-permute-start(f32[1024,128]{1,0:T(8,128)} %collective-permute-done.5), channel_id=1, source_target_pairs={{0,15},{1,0},{2,1},{3,2},{4,3},{5,4},{6,5},{7,6},{8,7},{9,8},{10,9... | collective-permute-start | bytes 1572872 | tf_op jit(solution)/shard_map/ppermute | solution.py:21
  89.5 13.3 %collective-permute-start.8 = (f32[1024,128]{1,0:T(8,128)}, f32[1024,128]{1,0:T(8,128)}, u32[]{:S(2)}, u32[]{:S(2)}) collective-permute-start(f32[1024,128]{1,0:T(8,128)} %collective-permute-done.6), channel_id=1, source_target_pairs={{0,1},{1,2},{2,3},{3,4},{4,5},{5,6},{6,7},{7,8},{8,9},{9,10},{10,1... | collective-permute-start | bytes 1572872 | tf_op jit(solution)/shard_map/ppermute | solution.py:16
  89.5 10.3 %copy-start.1 = (f32[4,1,1024,128]{3,2,1,0:T(8,128)S(1)}, f32[4,1,1024,128]{3,2,1,0:T(8,128)}, u32[]{:S(2)}) copy-start(f32[4,1,1024,128]{3,2,1,0:T(8,128)} %param.4) | copy-start | bytes 6291460
  89.6 18.0 %collective-permute-start.9 = (f32[1024,128]{1,0:T(8,128)}, f32[1024,128]{1,0:T(8,128)}, u32[]{:S(2)}, u32[]{:S(2)}) collective-permute-start(f32[1024,128]{1,0:T(8,128)} %collective-permute-done.7), channel_id=1, source_target_pairs={{0,15},{1,0},{2,1},{3,2},{4,3},{5,4},{6,5},{7,6},{8,7},{9,8},{10,9... | collective-permute-start | bytes 1572872 | tf_op jit(solution)/shard_map/ppermute | solution.py:21
  102.8 12.8 %collective-permute-start.10 = (f32[1024,128]{1,0:T(8,128)}, f32[1024,128]{1,0:T(8,128)}, u32[]{:S(2)}, u32[]{:S(2)}) collective-permute-start(f32[1024,128]{1,0:T(8,128)} %collective-permute-done.8), channel_id=1, source_target_pairs={{0,1},{1,2},{2,3},{3,4},{4,5},{5,6},{6,7},{7,8},{8,9},{9,10},{10,1... | collective-permute-start | bytes 1572872 | tf_op jit(solution)/shard_map/ppermute | solution.py:16
  107.6 14.7 %collective-permute-start.11 = (f32[1024,128]{1,0:T(8,128)}, f32[1024,128]{1,0:T(8,128)S(1)}, u32[]{:S(2)}, u32[]{:S(2)}) collective-permute-start(f32[1024,128]{1,0:T(8,128)} %collective-permute-done.9), channel_id=1, source_target_pairs={{0,15},{1,0},{2,1},{3,2},{4,3},{5,4},{6,5},{7,6},{8,7},{9,8},{10,9... | collective-permute-start | bytes 1572872 | tf_op jit(solution)/shard_map/ppermute | solution.py:21
  115.6 13.9 %collective-permute-start.12 = (f32[1024,128]{1,0:T(8,128)}, f32[1024,128]{1,0:T(8,128)S(1)}, u32[]{:S(2)}, u32[]{:S(2)}) collective-permute-start(f32[1024,128]{1,0:T(8,128)} %collective-permute-done.10), channel_id=1, source_target_pairs={{0,1},{1,2},{2,3},{3,4},{4,5},{5,6},{6,7},{7,8},{8,9},{9,10},{10,1... | collective-permute-start | bytes 1572872 | tf_op jit(solution)/shard_map/ppermute | solution.py:16
  122.3 12.8 %collective-permute-start.13 = (f32[1024,128]{1,0:T(8,128)S(1)}, f32[1024,128]{1,0:T(8,128)S(1)}, u32[]{:S(2)}, u32[]{:S(2)}) collective-permute-start(f32[1024,128]{1,0:T(8,128)S(1)} %collective-permute-done.11), channel_id=1, source_target_pairs={{0,15},{1,0},{2,1},{3,2},{4,3},{5,4},{6,5},{7,6},{8,7},{9,8},{10,9... | collective-permute-start | bytes 1572872 | tf_op jit(solution)/shard_map/ppermute | solution.py:21
  129.5 12.5 %collective-permute-start.14 = (f32[1024,128]{1,0:T(8,128)S(1)}, f32[1024,128]{1,0:T(8,128)S(1)}, u32[]{:S(2)}, u32[]{:S(2)}) collective-permute-start(f32[1024,128]{1,0:T(8,128)S(1)} %collective-permute-done.12), channel_id=1, source_target_pairs={{0,1},{1,2},{2,3},{3,4},{4,5},{5,6},{6,7},{7,8},{8,9},{9,10},{10,1... | collective-permute-start | bytes 1572872 | tf_op jit(solution)/shard_map/ppermute | solution.py:16
  252.9 4.3 copy-start
  278.8 214.8 %all-reduce.5.cloned.1.call-start = ((), (), s32[]{:S(2)}) async-start(), calls=%async_computation.5 | async-start | bytes 8388608 | tf_op jit(solution)/shard_map/psum | solution.py:30
  424.6 153.2 %reduce-scatter.5.cloned.1.call-start = ((), (), s32[]{:S(2)}) async-start(), calls=%async_computation.6 | async-start | bytes 4456448 | tf_op jit(solution)/shard_map/reduce_scatter | solution.py:38
  499.8 158.5 %reduce-scatter.7.cloned.1.call-start = ((), (), s32[]{:S(2)}) async-start(), calls=%async_computation.7 | async-start | bytes 4456448 | tf_op jit(solution)/shard_map/reduce_scatter | solution.py:38
  506.1 232.5 %reduce-scatter.9.cloned.1.call-start = ((), (), s32[]{:S(2)}) async-start(), calls=%async_computation.8 | async-start | bytes 4456448 | tf_op jit(solution)/shard_map/reduce_scatter | solution.py:38
  512.3 307.1 %reduce-scatter.11.cloned.1.call-start = ((), (), s32[]{:S(2)}) async-start(), calls=%async_computation.9 | async-start | bytes 4456448 | tf_op jit(solution)/shard_map/reduce_scatter | solution.py:38
  518.6 300.8 %copy-start.2 = (f32[4,1,64,1024]{3,2,1,0:T(8,128)S(1)}, f32[4,1,64,1024]{3,2,1,0:T(8,128)}, u32[]{:S(2)}) copy-start(f32[4,1,64,1024]{3,2,1,0:T(8,128)} %param.5) | copy-start | bytes 3145732
Sparse Core Ops, SparseCore 0:
  11.5 77.0 all-gather.2
  279.0 69.2 all-reduce.2
  424.7 68.8 all-reduce.4
  499.9 77.8 reduce-scatter.4
  581.3 76.9 reduce-scatter.6
  661.6 77.0 reduce-scatter.8
  742.3 77.0 reduce-scatter.10
